TPU v7x, 32 devices: a whole 2x2x4 slice. The times are simulated.
32 devices in a mesh: rows: 8 (over z, y), cols: 4 (over x, core).
Axes of the slice: x: 2, y: 2, z: 4, core: 2. Of those that a mesh axis runs over, the one named last changes fastest.
Arguments:
- factor: bfloat16 [4096, 256], P(('rows', 'cols')), may hold values from -0.09375 to 0.09375
- cores: bfloat16 [4, 256, 256], replicated, as said below
- tile_values: bfloat16 [4, 96, 512, 128], P(None, 'rows', 'cols'), may hold values from -56 to 56
- tile_rows: int32 [4, 8, 48], P(None, 'rows', 'cols'), may hold values from 0 to 3
- tile_cols: int32 [4, 8, 48], P(None, 'rows', 'cols'), may hold values from 0 to 7
- tile_counts: int32 [4, 8, 4], P(None, 'rows', 'cols'), may hold values from 3 to 12, as said below
Outputs:
- factor_new: bfloat16 [4096, 256], P(('rows', 'cols'))
- cores_new: float32 [4, 256, 256], replicated
Inputs may be any that keep to these rules, and one draw needn't show every extreme that they name: cores are dominated by their positive diagonals. `tile_counts`: every relation has some device whose 12 slots are all used. `tile_rows`: several slots may name the same tile.
All inputs are finite; a program needn't handle non-finite values.
Results may differ from a plain program's by a relative error of at most 0.0034.
The roundings to bfloat16 on the way count: a program that leaves them out, or rounds other values in their place, can miss the bound.
Values may be sent and summed in bfloat16 or wider, within the bound.
No kernel may reach another device: no remote copies, remote signals or barrier semaphores. Data moves between devices by JAX's collectives and lax.ppermute only.
A program may use at most 128 MiB of HBM per device.

v0:
```python
import jax
import jax.numpy as jnp
from jax import lax
from jax.sharding import PartitionSpec as P

ridge_weight = 0.1


def normal_system(summed_gram_matrix, cores_float32):
    direct_part = jnp.einsum(
        "krs,st,kqt->rq",
        cores_float32,
        summed_gram_matrix,
        cores_float32,
        precision=lax.Precision.HIGHEST,
    )
    reflected_part = jnp.einsum(
        "euh,uc,eca->ha",
        cores_float32,
        summed_gram_matrix,
        cores_float32,
        precision=lax.Precision.HIGHEST,
    )
    return (
        direct_part
        + reflected_part
        + ridge_weight * jnp.eye(summed_gram_matrix.shape[0], dtype=jnp.float32)
    )


def solve_rows(cholesky_lhs, numerator):
    halfway = lax.linalg.triangular_solve(cholesky_lhs, numerator.T, left_side=True, lower=True)
    return lax.linalg.triangular_solve(
        cholesky_lhs, halfway, left_side=True, lower=True, transpose_a=True
    ).T


def whiten(cholesky_new, core_num):
    relations, rank_size, _ = core_num.shape
    stacked = core_num.transpose(1, 0, 2).reshape(rank_size, relations * rank_size)
    halfway = lax.linalg.triangular_solve(cholesky_new, stacked, left_side=True, lower=True)
    flipped = (
        halfway.reshape(rank_size, relations, rank_size)
        .transpose(2, 1, 0)
        .reshape(rank_size, relations * rank_size)
    )
    second = lax.linalg.triangular_solve(cholesky_new, flipped, left_side=True, lower=True)
    return second.reshape(rank_size, relations, rank_size).transpose(1, 2, 0)


def local(factor, cores, tile_values, tile_rows, tile_cols, tile_counts):
    relations, slot_count, tile_size, _ = tile_values.shape
    own_rows, rank_size = factor.shape
    row_ids = tile_rows[:, 0, :]
    col_ids = tile_cols[:, 0, :]
    live_mask = (jnp.arange(slot_count, dtype=jnp.int32)[None, :] < tile_counts[:, 0, :]).astype(
        jnp.float32
    )
    cores_float32 = cores.astype(jnp.float32)
    gram_old = lax.psum(
        jnp.dot(factor.T, factor, preferred_element_type=jnp.float32), ("rows", "cols")
    )
    cholesky_lhs = jnp.linalg.cholesky(normal_system(gram_old, cores_float32))
    col_tiles = lax.all_gather(factor, "rows", axis=0, tiled=True).reshape(-1, tile_size, rank_size)
    col_count = col_tiles.shape[0]
    panel_tiles = lax.axis_size("cols") * own_rows // tile_size
    row_partial = jnp.zeros((panel_tiles, tile_size, relations, rank_size), jnp.float32)
    for relation in range(relations):
        products = jnp.einsum(
            "sij,sjr->sir",
            tile_values[relation],
            col_tiles[col_ids[relation]],
            preferred_element_type=jnp.float32,
        )
        products = products * live_mask[relation][:, None, None]
        row_partial = row_partial.at[row_ids[relation], :, relation].add(products)
    row_partial = row_partial.reshape(panel_tiles * tile_size, relations, rank_size)
    flat_partial = row_partial.reshape(panel_tiles * tile_size, relations * rank_size)
    row_sum = lax.psum_scatter(flat_partial, "cols", scatter_dimension=0, tiled=True)
    direct = row_sum.reshape(own_rows, relations, rank_size)
    numerator = jnp.einsum("eks,kqs->eq", direct, cores_float32, precision=lax.Precision.HIGHEST)
    panel = lax.all_gather(factor, "cols", axis=0, tiled=True)
    rotated = jnp.einsum("pr,krs->pks", panel, cores, preferred_element_type=jnp.float32).astype(
        jnp.bfloat16
    )
    rotated_tiles = rotated.reshape(panel_tiles, tile_size, relations, rank_size)
    col_partial = jnp.zeros((col_count, tile_size, rank_size), jnp.float32)
    for relation in range(relations):
        rotated_selection = rotated_tiles[row_ids[relation], :, relation]
        back_products = jnp.einsum(
            "sij,sir->sjr",
            tile_values[relation],
            rotated_selection,
            preferred_element_type=jnp.float32,
        )
        back_products = back_products * live_mask[relation][:, None, None]
        col_partial = col_partial.at[col_ids[relation]].add(back_products)
    col_partial = col_partial.reshape(col_count * tile_size, rank_size)
    numerator = numerator + lax.psum_scatter(col_partial, "rows", scatter_dimension=0, tiled=True)
    factor_new = solve_rows(cholesky_lhs, numerator).astype(jnp.bfloat16)
    gram_part = jnp.dot(factor_new.T, factor_new, preferred_element_type=jnp.float32)
    col_new = lax.all_gather(factor_new, "rows", axis=0, tiled=True).reshape(
        -1, tile_size, rank_size
    )
    panel_new = lax.all_gather(factor_new, "cols", axis=0, tiled=True).reshape(
        -1, tile_size, rank_size
    )
    core_matrices = []
    for relation in range(relations):
        upper = jnp.einsum(
            "sij,sir->sjr",
            tile_values[relation],
            panel_new[row_ids[relation]],
            preferred_element_type=jnp.float32,
        ).astype(jnp.bfloat16)
        upper = jnp.where(live_mask[relation][:, None, None] > 0, upper, jnp.zeros_like(upper))
        core_matrices.append(
            jnp.einsum(
                "sjr,sjq->rq", upper, col_new[col_ids[relation]], preferred_element_type=jnp.float32
            )
        )
    core_part = jnp.stack(core_matrices, axis=0)
    gram_new = lax.psum(gram_part, ("rows", "cols"))
    core_num = lax.psum(core_part, ("rows", "cols"))
    cores_new = whiten(jnp.linalg.cholesky(gram_new), core_num)
    return (factor_new, cores_new)


def solution(mesh):
    in_specs = (
        P(("rows", "cols"), None),
        P(),
        P(None, "rows", "cols", None),
        P(None, "rows", "cols"),
        P(None, "rows", "cols"),
        P(None, "rows", "cols"),
    )
    out_specs = (P(("rows", "cols"), None), P())
    return jax.shard_map(local, mesh=mesh, in_specs=in_specs, out_specs=out_specs, check_vma=False)
```

profile of v0, /device:TPU:0, one launch (start us, length us, event | category | flops | bytes accessed | tf_op | source)
XLA Modules:
  0.0 483.6 jit_solution(10696427226409059928)
XLA Ops:
  10.0 33.4 %all_gather.12 = bf16[1024,256]{1,0:T(8,128)(2,1)S(1)} all-gather(bf16[128,256]{1,0:T(8,128)(2,1)} %param.9), channel_id=1, replica_groups=mesh['rows'=8,'cols'=4] {'rows'}, dimensions={0}, use_global_device_ids=true | all-gather | bytes 589824 | tf_op jit(solution)/shard_map/all_gather | solution.py:64
  59.0 3.1 copy.37
  63.8 3.0 copy.41
  67.1 3.2 scatter_fusion
  70.2 3.2 scatter_fusion.1
  73.4 3.2 scatter_fusion.2
  76.6 3.2 scatter_fusion.3
  83.8 6.0 %all_gather.13 = bf16[512,256]{1,0:T(8,128)(2,1)S(1)} all-gather(bf16[128,256]{1,0:T(8,128)(2,1)S(1)} %copy-done.9), channel_id=1, replica_groups=mesh['rows'=8,'cols'=4] {'cols'}, dimensions={0}, use_global_device_ids=true | all-gather | bytes 327680 | tf_op jit(solution)/shard_map/all_gather | solution.py:82
  90.9 2.7 multiply_bitcast_fusion.3
  97.0 2.8 multiply_bitcast_fusion.2
  99.8 3.1 copy.50
  104.5 2.9 multiply_bitcast_fusion.1
  107.4 3.1 copy.53
  111.9 2.8 multiply_bitcast_fusion
  114.7 3.1 copy.56
  119.8 3.1 scatter_fusion.5
  124.8 3.1 scatter_fusion.7
  129.5 22.2 %all-reduce.9.cloned.1.call-done = f32[256,256]{1,0:T(8,128)} async-done(((f32[256,256]{1,0:T(8,128)}), f32[256,256]{1,0:T(8,128)}) %all-reduce.9.cloned.1.call-update) | async-done | bytes 262160 | tf_op jit(solution)/shard_map/psum | solution.py:60
  155.7 11.7 %cholesky.130 = f32[128,128]{1,0:T(8,128)S(1)} custom-call(f32[128,128]{1,0:T(8,128)S(1)} %cholesky.194), custom_call_target="Cholesky" | custom-call | tf_op jit(solution)/shard_map/jit(cholesky)/cholesky | solution.py:63
  167.6 9.8 %custom-call.35 = f32[1,128,128]{1,2,0:T(8,128)S(1)} custom-call(f32[1,128,128]{2,1,0:T(8,128)S(1)} %get-tuple-element.75), custom_call_target="InvertDiagBlocksLowerTriangular" | custom-call | tf_op jit(solution)/shard_map/jit(cholesky)/cholesky | solution.py:63
  178.0 11.9 %cholesky.147 = f32[128,128]{1,0:T(8,128)S(1)} custom-call(f32[128,128]{1,0:T(8,128)S(1)} %convolution_subtract_fusion.5), custom_call_target="Cholesky" | custom-call | tf_op jit(solution)/shard_map/jit(cholesky)/cholesky | solution.py:63
  192.2 4.4 while.5
  196.6 19.7 %custom-call.16 = f32[2,128,128]{1,2,0:T(8,128)S(1)} custom-call(f32[2,128,128]{2,1,0:T(8,128)S(1)} %get-tuple-element.19), custom_call_target="InvertDiagBlocksLowerTriangular" | custom-call | tf_op jit(solution)/shard_map/triangular_solve | solution.py:33
  221.5 27.7 %all_gather.15 = bf16[1024,256]{0,1:T(8,128)(2,1)S(1)} all-gather(bf16[128,256]{0,1:T(8,128)(2,1)S(1)} %fusion.88), channel_id=1, replica_groups=mesh['rows'=8,'cols'=4] {'rows'}, dimensions={0}, use_global_device_ids=true | all-gather | bytes 589824 | tf_op jit(solution)/shard_map/all_gather | solution.py:102
  249.2 5.8 %all_gather.14 = bf16[512,256]{0,1:T(8,128)(2,1)S(1)} all-gather(bf16[128,256]{0,1:T(8,128)(2,1)S(1)} %fusion.88), channel_id=1, replica_groups=mesh['rows'=8,'cols'=4] {'cols'}, dimensions={0}, use_global_device_ids=true | all-gather | bytes 327680 | tf_op jit(solution)/shard_map/all_gather | solution.py:105
  270.6 2.8 fusion.14
  278.7 128.2 %all-reduce.11.cloned.1.call-done = (f32[256,1024]{0,1:T(8,128)}, f32[256,256]{0,1:T(8,128)}) async-done(((f32[256,1024]{0,1:T(8,128)}, f32[256,256]{0,1:T(8,128)}), (f32[256,1024]{0,1:T(8,128)}, f32[256,256]{0,1:T(8,128)})) %all-reduce.11.cloned.1.call-update) | async-done | bytes 1310736 | tf_op jit(solution)/shard_map/psum | solution.py:124
  409.0 11.7 %cholesky.164 = f32[128,128]{1,0:T(8,128)S(1)} custom-call(f32[128,128]{1,0:T(8,128)S(1)} %cholesky.197), custom_call_target="Cholesky" | custom-call | tf_op jit(solution)/shard_map/jit(cholesky)/cholesky | solution.py:125
  420.8 9.8 %custom-call.36 = f32[1,128,128]{1,2,0:T(8,128)S(1)} custom-call(f32[1,128,128]{2,1,0:T(8,128)S(1)} %get-tuple-element.73), custom_call_target="InvertDiagBlocksLowerTriangular" | custom-call | tf_op jit(solution)/shard_map/jit(cholesky)/cholesky | solution.py:125
  431.1 11.9 %cholesky.181 = f32[128,128]{1,0:T(8,128)S(1)} custom-call(f32[128,128]{1,0:T(8,128)S(1)} %convolution_subtract_fusion.2), custom_call_target="Cholesky" | custom-call | tf_op jit(solution)/shard_map/jit(cholesky)/cholesky | solution.py:125
  445.7 4.1 while.6
  449.8 19.7 %custom-call.38 = f32[2,128,128]{1,2,0:T(8,128)S(1)} custom-call(f32[2,128,128]{2,1,0:T(8,128)S(1)} %get-tuple-element.27), custom_call_target="InvertDiagBlocksLowerTriangular" | custom-call | tf_op jit(solution)/shard_map/triangular_solve/custom-call.5 | solution.py:47
  (156 shorter events, 86.5 us)
Async XLA Ops:
  8.0 81.8 %copy-start = (bf16[4,256,256]{2,1,0:T(8,128)(2,1)S(1)}, bf16[4,256,256]{2,1,0:T(8,128)(2,1)}, u32[]{:S(2)}) copy-start(bf16[4,256,256]{2,1,0:T(8,128)(2,1)} %param.10) | copy-start | bytes 1572868
  8.0 143.7 %all-reduce.9.cloned.1.call-start = ((), (), s32[]{:S(2)}) async-start(), calls=%async_computation.2 | async-start | bytes 524288 | tf_op jit(solution)/shard_map/psum | solution.py:60
  9.9 206.4 %reduce-scatter.3.cloned.1.call-start = ((), (), s32[]{:S(2)}) async-start(), calls=%async_computation.3 | async-start | bytes 2621440 | tf_op jit(solution)/shard_map/reduce_scatter | solution.py:79
  50.7 1.8 copy-start.4
  50.8 2.0 copy-start.6
  52.6 1.7 copy-start.7
  59.0 3.1 copy-start.3
  82.9 0.8 copy-start.9
  82.9 134.6 %reduce-scatter.5.cloned.1.call-start = ((), (), s32[]{:S(2)}) async-start(), calls=%async_computation.4 | async-start | bytes 1179648 | tf_op jit(solution)/shard_map/reduce_scatter | solution.py:99
  119.8 3.1 copy-start.2
  127.9 1.0 copy-start.1
  128.9 278.0 %all-reduce.11.cloned.1.call-start = ((), (), s32[]{:S(2)}) async-start(), calls=%async_computation.5 | async-start | bytes 2621440 | tf_op jit(solution)/shard_map/psum | solution.py:124
  151.7 2.5 copy-start.8
  263.4 3.0 copy-start.5
  409.0 60.6 %copy-start.10 = (f32[256,1024]{0,1:T(8,128)S(1)}, f32[256,1024]{0,1:T(8,128)}, u32[]{:S(2)}) copy-start(f32[256,1024]{0,1:T(8,128)} %get-tuple-element.56) | copy-start | bytes 3145732
Sparse Core Ops, SparseCore 0:
  14.3 137.2 all-reduce.8
  278.1 128.7 all-reduce.10
Sparse Core Ops, SparseCore 1:
  83.0 32.4 reduce-scatter.2
  129.0 64.6 reduce-scatter.4
where the time goes:
time: 492 us; the launch traced here: 484 us
  waiting for transfers between devices  150 us (30%)
  other arithmetic  137 us (28%)
  blocking collectives  72.9 us (15%)
  local copies, waits for them, and re-layouts  61.2 us (12%)
  matrix products  42.5 us (9%)
  between operations  19.3 us (4%)
    psum x1, waiting for transfers between devices, local(): core_num = lax.psum(core_part, ('rows', 'cols'))  128 us
    another operation x7, other arithmetic, local(): cores_new = whiten(jnp.linalg.cholesky(gram_new), core_num)  34.8 us
    another operation x6, other arithmetic, local(): cholesky_lhs = jnp.linalg.cholesky(normal_system(gram_old, cores_float32))  34.2 us
    all_gather x1, blocking collectives, local(): lax.all_gather(factor, 'rows', axis=0, tiled=True)  33.4 us
    all_gather x1, blocking collectives, local(): lax.all_gather(factor_new, 'rows', axis=0, tiled=True)  27.7 us
    psum x1, waiting for transfers between devices, local(): lax.psum(jnp.dot(factor.T, factor, preferred_element_type=jnp.float32), (...  22.2 us
    another operation x3, other arithmetic, whiten(): lax.linalg.triangular_solve(cholesky_new, flipped, left_side=True, lower=...  19.8 us
    another operation x3, other arithmetic, solve_rows(): lax.linalg.triangular_solve(cholesky_lhs, halfway, left_side=True, lower=...  19.7 us
  transfers between devices with their start and end apart: 4, of which 2 were waited for; matrix products, arithmetic and copies ran while one was open for 29% of the time, Pallas kernels for 0%

commit v1 on v0

--- a/solution.py
+++ b/solution.py
@@ -121,7 +121,7 @@
         )
     core_part = jnp.stack(core_matrices, axis=0)
     gram_new = lax.psum(gram_part, ("rows", "cols"))
-    core_num = lax.psum(core_part, ("rows", "cols"))
+    core_num = lax.psum(lax.psum(core_part, "cols"), "rows")
     cores_new = whiten(jnp.linalg.cholesky(gram_new), core_num)
     return (factor_new, cores_new)
 

time: 492 us -> 528 us (1.073)
  waiting for transfers between devices: 150 us -> 182 us
    psum x1 -> x3, waiting for transfers between devices: 128 us -> 159 us  [the longest x1 105 us: local(): gram_new = lax.psum(gram_part, ('rows', 'cols'))]
  transfers between devices with their start and end apart: 4 -> 6, of which waited for: 2 -> 4; matrix products, arithmetic and copies ran while one was open for 29% -> 42% of each run, Pallas kernels for 0% -> 0%
where the time goes in v1:
time: 528 us; the launch traced here: 519 us
  waiting for transfers between devices  182 us (34%)
  other arithmetic  136 us (26%)
  blocking collectives  72.9 us (14%)
  local copies, waits for them, and re-layouts  63.7 us (12%)
  matrix products  44.4 us (8%)
  between operations  19.1 us (4%)
    psum x1, waiting for transfers between devices, local(): gram_new = lax.psum(gram_part, ('rows', 'cols'))  105 us
    psum x2, waiting for transfers between devices, local(): core_num = lax.psum(lax.psum(core_part, 'cols'), 'rows')  54.5 us
    another operation x7, other arithmetic, local(): cores_new = whiten(jnp.linalg.cholesky(gram_new), core_num)  34.7 us
    another operation x6, other arithmetic, local(): cholesky_lhs = jnp.linalg.cholesky(normal_system(gram_old, cores_float32))  34.2 us
    all_gather x1, blocking collectives, local(): lax.all_gather(factor, 'rows', axis=0, tiled=True)  33.4 us
    all_gather x1, blocking collectives, local(): lax.all_gather(factor_new, 'rows', axis=0, tiled=True)  27.6 us
    psum x1, waiting for transfers between devices, local(): lax.psum(jnp.dot(factor.T, factor, preferred_element_type=jnp.float32), (...  22.2 us
    another operation x3, other arithmetic, whiten(): lax.linalg.triangular_solve(cholesky_new, flipped, left_side=True, lower=...  19.8 us
  transfers between devices with their start and end apart: 6, of which 4 were waited for; matrix products, arithmetic and copies ran while one was open for 42% of the time, Pallas kernels for 0%

profile of v1, /device:TPU:0, one launch (start us, length us, event | category | flops | bytes accessed | tf_op | source)
XLA Modules:
  0.0 519.2 jit_solution(7781579864940370629)
XLA Ops:
  10.0 33.4 %all_gather.12 = bf16[1024,256]{1,0:T(8,128)(2,1)S(1)} all-gather(bf16[128,256]{1,0:T(8,128)(2,1)} %param.9), channel_id=1, replica_groups=mesh['rows'=8,'cols'=4] {'rows'}, dimensions={0}, use_global_device_ids=true | all-gather | bytes 589824 | tf_op jit(solution)/shard_map/all_gather | solution.py:64
  59.0 3.1 copy.37
  63.8 3.0 copy.41
  67.1 3.2 scatter_fusion
  70.2 3.2 scatter_fusion.1
  73.4 3.2 scatter_fusion.2
  76.6 3.2 scatter_fusion.3
  83.8 6.0 %all_gather.13 = bf16[512,256]{1,0:T(8,128)(2,1)S(1)} all-gather(bf16[128,256]{1,0:T(8,128)(2,1)S(1)} %copy-done.9), channel_id=1, replica_groups=mesh['rows'=8,'cols'=4] {'cols'}, dimensions={0}, use_global_device_ids=true | all-gather | bytes 327680 | tf_op jit(solution)/shard_map/all_gather | solution.py:82
  97.0 2.8 multiply_bitcast_fusion.2
  99.8 3.1 copy.50
  104.5 2.9 multiply_bitcast_fusion.1
  107.3 3.1 copy.53
  111.9 2.8 multiply_bitcast_fusion
  114.7 3.1 copy.56
  119.8 3.1 scatter_fusion.5
  124.8 3.1 scatter_fusion.7
  129.4 22.2 %all-reduce.10.cloned.1.call-done = f32[256,256]{1,0:T(8,128)} async-done(((f32[256,256]{1,0:T(8,128)}), f32[256,256]{1,0:T(8,128)}) %all-reduce.10.cloned.1.call-update) | async-done | bytes 262160 | tf_op jit(solution)/shard_map/psum | solution.py:60
  155.7 11.7 %cholesky.130 = f32[128,128]{1,0:T(8,128)S(1)} custom-call(f32[128,128]{1,0:T(8,128)S(1)} %cholesky.194), custom_call_target="Cholesky" | custom-call | tf_op jit(solution)/shard_map/jit(cholesky)/cholesky | solution.py:63
  167.5 9.8 %custom-call.35 = f32[1,128,128]{1,2,0:T(8,128)S(1)} custom-call(f32[1,128,128]{2,1,0:T(8,128)S(1)} %get-tuple-element.73), custom_call_target="InvertDiagBlocksLowerTriangular" | custom-call | tf_op jit(solution)/shard_map/jit(cholesky)/cholesky | solution.py:63
  178.0 11.9 %cholesky.147 = f32[128,128]{1,0:T(8,128)S(1)} custom-call(f32[128,128]{1,0:T(8,128)S(1)} %convolution_subtract_fusion.5), custom_call_target="Cholesky" | custom-call | tf_op jit(solution)/shard_map/jit(cholesky)/cholesky | solution.py:63
  192.2 4.4 while.5
  196.6 19.7 %custom-call.16 = f32[2,128,128]{1,2,0:T(8,128)S(1)} custom-call(f32[2,128,128]{2,1,0:T(8,128)S(1)} %get-tuple-element.19), custom_call_target="InvertDiagBlocksLowerTriangular" | custom-call | tf_op jit(solution)/shard_map/triangular_solve | solution.py:33
  221.5 27.6 %all_gather.15 = bf16[1024,256]{0,1:T(8,128)(2,1)S(1)} all-gather(bf16[128,256]{0,1:T(8,128)(2,1)S(1)} %fusion.88), channel_id=1, replica_groups=mesh['rows'=8,'cols'=4] {'rows'}, dimensions={0}, use_global_device_ids=true | all-gather | bytes 589824 | tf_op jit(solution)/shard_map/all_gather | solution.py:102
  249.1 5.8 %all_gather.14 = bf16[512,256]{0,1:T(8,128)(2,1)S(1)} all-gather(bf16[128,256]{0,1:T(8,128)(2,1)S(1)} %fusion.88), channel_id=1, replica_groups=mesh['rows'=8,'cols'=4] {'cols'}, dimensions={0}, use_global_device_ids=true | all-gather | bytes 327680 | tf_op jit(solution)/shard_map/all_gather | solution.py:105
  278.9 104.7 %all-reduce.12.cloned.1.call-done = f32[256,256]{0,1:T(8,128)} async-done(((f32[256,256]{0,1:T(8,128)}), f32[256,256]{0,1:T(8,128)}) %all-reduce.12.cloned.1.call-update) | async-done | bytes 262160 | tf_op jit(solution)/shard_map/psum | solution.py:123
  385.6 11.7 %cholesky.164 = f32[128,128]{1,0:T(8,128)S(1)} custom-call(f32[128,128]{1,0:T(8,128)S(1)} %cholesky.197), custom_call_target="Cholesky" | custom-call | tf_op jit(solution)/shard_map/jit(cholesky)/cholesky | solution.py:125
  397.4 9.8 %custom-call.36 = f32[1,128,128]{1,2,0:T(8,128)S(1)} custom-call(f32[1,128,128]{2,1,0:T(8,128)S(1)} %get-tuple-element.71), custom_call_target="InvertDiagBlocksLowerTriangular" | custom-call | tf_op jit(solution)/shard_map/jit(cholesky)/cholesky | solution.py:125
  407.7 11.7 %cholesky.181 = f32[128,128]{1,0:T(8,128)S(1)} custom-call(f32[128,128]{1,0:T(8,128)S(1)} %convolution_subtract_fusion.2), custom_call_target="Cholesky" | custom-call | tf_op jit(solution)/shard_map/jit(cholesky)/cholesky | solution.py:125
  419.4 3.1 all-reduce.14.cloned.1.call-done
  427.7 4.3 while.6
  432.1 19.7 %custom-call.38 = f32[2,128,128]{1,2,0:T(8,128)S(1)} custom-call(f32[2,128,128]{2,1,0:T(8,128)S(1)} %get-tuple-element.27), custom_call_target="InvertDiagBlocksLowerTriangular" | custom-call | tf_op jit(solution)/shard_map/triangular_solve/custom-call.5 | solution.py:47
  451.8 51.4 %all-reduce.16.cloned.1.call-done = f32[256,1024]{0,1:T(8,128)} async-done(((f32[256,1024]{0,1:T(8,128)}), f32[256,1024]{0,1:T(8,128)}) %all-reduce.16.cloned.1.call-update) | async-done | bytes 1048592 | tf_op jit(solution)/shard_map/psum | solution.py:124
  (161 shorter events, 96.6 us)
Async XLA Ops:
  8.0 81.8 %copy-start = (bf16[4,256,256]{2,1,0:T(8,128)(2,1)S(1)}, bf16[4,256,256]{2,1,0:T(8,128)(2,1)}, u32[]{:S(2)}) copy-start(bf16[4,256,256]{2,1,0:T(8,128)(2,1)} %param.10) | copy-start | bytes 1572868
  8.0 143.6 %all-reduce.10.cloned.1.call-start = ((), (), s32[]{:S(2)}) async-start(), calls=%async_computation.2 | async-start | bytes 524288 | tf_op jit(solution)/shard_map/psum | solution.py:60
  9.9 206.4 %reduce-scatter.3.cloned.1.call-start = ((), (), s32[]{:S(2)}) async-start(), calls=%async_computation.3 | async-start | bytes 2621440 | tf_op jit(solution)/shard_map/reduce_scatter | solution.py:79
  50.7 1.8 copy-start.4
  50.8 2.0 copy-start.6
  52.6 1.7 copy-start.7
  59.0 3.1 copy-start.3
  82.9 0.8 copy-start.9
  82.9 134.6 %reduce-scatter.5.cloned.1.call-start = ((), (), s32[]{:S(2)}) async-start(), calls=%async_computation.4 | async-start | bytes 1179648 | tf_op jit(solution)/shard_map/reduce_scatter | solution.py:99
  119.8 3.1 copy-start.2
  127.9 1.0 copy-start.1
  128.9 254.7 %all-reduce.12.cloned.1.call-start = ((), (), s32[]{:S(2)}) async-start(), calls=%async_computation.5 | async-start | bytes 524288 | tf_op jit(solution)/shard_map/psum | solution.py:123
  151.7 2.5 copy-start.8
  261.1 161.5 %all-reduce.14.cloned.1.call-start = ((), (), s32[]{:S(2)}) async-start(), calls=%async_computation.6 | async-start | bytes 2097152 | tf_op jit(solution)/shard_map/psum | solution.py:124
  264.3 3.0 copy-start.5
  278.6 224.5 %all-reduce.16.cloned.1.call-start = ((), (), s32[]{:S(2)}) async-start(), calls=%async_computation.7 | async-start | bytes 2097152 | tf_op jit(solution)/shard_map/psum | solution.py:124
Sparse Core Ops, SparseCore 0:
  14.3 137.2 all-reduce.9
  261.2 122.3 all-reduce.11
  386.5 35.9 all-reduce.13
Sparse Core Ops, SparseCore 1:
  83.0 32.4 reduce-scatter.2
  129.0 64.7 reduce-scatter.4
  425.2 77.9 all-reduce.15
